TPU v7x, 32 devices: a whole 2x2x4 slice. The times are simulated.
32 devices in a mesh: dp: 8 (over z, core), row: 2 (over x), col: 2 (over y).
Axes of the slice: x: 2, y: 2, z: 4, core: 2. Of those that a mesh axis runs over, the one named last changes fastest.
Arguments:
- tokens: bfloat16 [16384, 1024], P(('dp', 'row'), 'col'), may hold values from -6 to 6
- mixer_gain: float32 [1024], P('col'), may hold values from 0.1 to 1.9
- in_weight: bfloat16 [1024, 3, 1024], P('col', None, 'row'), may hold values from -0.1875 to 0.1875
- conv_kernel: float32 [3, 1024], P(None, 'row'), may hold values from -3.5 to 3.5
- out_weight: bfloat16 [1024, 1024], P('row', 'col'), may hold values from -0.1875 to 0.1875
- ffn_gain: float32 [1024], P('col'), may hold values from 0.1 to 1.9
- ffn_weight: bfloat16 [1024, 2, 4608], P('col', None, 'row'), may hold values from -0.1875 to 0.1875
- down_weight: bfloat16 [4608, 1024], P('row', 'col'), may hold values from -0.1875 to 0.1875
- cotangent: bfloat16 [16384, 1024], P(('dp', 'row'), 'col'), may hold values from -6 to 6
Outputs:
- output: bfloat16 [16384, 1024], P(('dp', 'row'), 'col')
- d_tokens: float32 [16384, 1024], P(('dp', 'row'), 'col')
- d_mixer_gain: float32 [1024], P('col')
- d_in_weight: float32 [1024, 3, 1024], P('col', None, 'row')
- d_conv_kernel: float32 [3, 1024], P(None, 'row')
- d_out_weight: float32 [1024, 1024], P('row', 'col')
- d_ffn_gain: float32 [1024], P('col')
- d_ffn_weight: float32 [1024, 2, 4608], P('col', None, 'row')
- d_down_weight: float32 [4608, 1024], P('row', 'col')
All inputs are finite; a program needn't handle non-finite values.
Results may differ from a plain program's by a relative error of at most 0.015.
Values may be sent and summed in bfloat16 or wider, within the bound.
No kernel may reach another device: no remote copies, remote signals or barrier semaphores. Data moves between devices by JAX's collectives and lax.ppermute only.
A program may use at most 320 MiB of HBM per device.

v0:
```python
import jax
import jax.numpy as jnp
from jax import lax
from jax.sharding import PartitionSpec as P

D = 1024
EPS = 1e-05


def shifted(block, axis, distance):
    devices = range(lax.axis_size(axis))
    route = [(i - distance, i) for i in devices if i - distance in devices]
    return lax.ppermute(block, axis, route)


def dense(left, matrix, transposed):
    if transposed:
        return lax.dot_general(
            left, matrix, (((1,), (1,)), ((), ())), preferred_element_type=jnp.float32
        )
    return jnp.dot(left, matrix, preferred_element_type=jnp.float32)


def grads_of(left, right):
    return lax.dot_general(
        left, right, (((0,), (0,)), ((), ())), preferred_element_type=jnp.float32
    )


def tokens_by_row(value):
    return lax.all_gather(value, "row", axis=0, tiled=True)


def tokens_by_col(value):
    return lax.all_gather(value, "col", axis=0, tiled=True)


def spread_wide(gathered, matrix, transposed):
    height = gathered.shape[0] // lax.axis_size("col")

    def partial_rows(start, count):
        return dense(gathered, matrix, transposed)

    return lax.psum_scatter(
        partial_rows(jnp.int32(0), height * lax.axis_size("col")),
        "col",
        scatter_dimension=0,
        tiled=True,
    )


def spread_narrow(gathered, matrix, transposed):
    height = gathered.shape[0] // lax.axis_size("row")

    def partial_rows(start, count):
        return dense(gathered, matrix, transposed)

    return lax.psum_scatter(
        partial_rows(jnp.int32(0), height * lax.axis_size("row")),
        "row",
        scatter_dimension=0,
        tiled=True,
    )


def width_total(value):
    return lax.psum(value, "col")


def local(
    tokens,
    mixer_gain,
    in_weight,
    conv_kernel,
    out_weight,
    ffn_gain,
    ffn_weight,
    down_weight,
    cotangent,
):
    xfloat = tokens.astype(jnp.float32)
    scale_one = lax.rsqrt(width_total(jnp.sum(xfloat * xfloat, axis=1, keepdims=True)) / D + EPS)
    normed_one = xfloat * scale_one
    hidden_one = (normed_one * mixer_gain).astype(jnp.bfloat16)
    wide_in = in_weight.reshape(in_weight.shape[0], -1)
    gathered_one = tokens_by_row(hidden_one)
    projected = spread_wide(gathered_one, wide_in, False)
    block_width = conv_kernel.shape[1]
    gate_b = projected[:, :block_width]
    gate_c = projected[:, block_width : 2 * block_width]
    values = projected[:, 2 * block_width :]
    mixed_in = gate_b * values
    previous = shifted(mixed_in[-2:], "col", 1)
    extended = jnp.concatenate([previous, mixed_in], 0)
    lag_one = extended[1:-1]
    lag_two = extended[:-2]
    convolved = conv_kernel[2] * mixed_in + conv_kernel[1] * lag_one + conv_kernel[0] * lag_two
    mixer_out = (gate_c * convolved).astype(jnp.bfloat16)
    gathered_mix = tokens_by_col(mixer_out)
    residual = xfloat + spread_narrow(gathered_mix, out_weight, False)
    scale_two = lax.rsqrt(
        width_total(jnp.sum(residual * residual, axis=1, keepdims=True)) / D + EPS
    )
    normed_two = residual * scale_two
    hidden_two = (normed_two * ffn_gain).astype(jnp.bfloat16)
    wide_ffn = ffn_weight.reshape(ffn_weight.shape[0], -1)
    gathered_two = tokens_by_row(hidden_two)
    gate_up = spread_wide(gathered_two, wide_ffn, False)
    inner_width = down_weight.shape[0]
    gate_part = gate_up[:, :inner_width]
    up_part = gate_up[:, inner_width:]
    sigmoid_gate = jax.nn.sigmoid(gate_part)
    activated = (gate_part * sigmoid_gate * up_part).astype(jnp.bfloat16)
    gathered_act = tokens_by_col(activated)
    output = (residual + spread_narrow(gathered_act, down_weight, False)).astype(jnp.bfloat16)
    cot_rows = tokens_by_row(cotangent)
    d_act = spread_wide(cot_rows, down_weight, True)
    grad_down = grads_of(gathered_act, cot_rows)
    d_gate = d_act * up_part * sigmoid_gate * (1.0 + gate_part * (1.0 - sigmoid_gate))
    d_up = d_act * gate_part * sigmoid_gate
    d_gate_up = jnp.concatenate([d_gate, d_up], 1).astype(jnp.bfloat16)
    dgu_rows = tokens_by_col(d_gate_up)
    d_hidden_two = spread_narrow(dgu_rows, wide_ffn, True)
    grad_ffn = grads_of(gathered_two, dgu_rows).reshape(ffn_weight.shape)
    scaled_two = d_hidden_two * ffn_gain
    inner_two = width_total(jnp.sum(scaled_two * normed_two, axis=1, keepdims=True)) / D
    d_residual = cotangent.astype(jnp.float32) + scale_two * (scaled_two - normed_two * inner_two)
    gain_two_part = jnp.sum(d_hidden_two * normed_two, axis=0)
    d_residual_b = d_residual.astype(jnp.bfloat16)
    dres_rows = tokens_by_row(d_residual_b)
    d_mix = spread_wide(dres_rows, out_weight, True)
    grad_out = grads_of(gathered_mix, dres_rows)
    d_gate_c = d_mix * convolved
    d_conv = d_mix * gate_c
    following = shifted(d_conv[:2], "col", -1)
    ahead_rows = jnp.concatenate([d_conv, following], 0)
    d_mixed = (
        conv_kernel[2] * d_conv
        + conv_kernel[1] * ahead_rows[1:-1]
        + conv_kernel[0] * ahead_rows[2:]
    )
    kernel_part = jnp.stack(
        [
            jnp.sum(d_conv * lag_two, axis=0),
            jnp.sum(d_conv * lag_one, axis=0),
            jnp.sum(d_conv * mixed_in, axis=0),
        ]
    )
    d_projected = jnp.concatenate([d_mixed * values, d_gate_c, d_mixed * gate_b], 1).astype(
        jnp.bfloat16
    )
    dproj_rows = tokens_by_col(d_projected)
    d_hidden_one = spread_narrow(dproj_rows, wide_in, True)
    grad_in = grads_of(gathered_one, dproj_rows).reshape(in_weight.shape)
    scaled_one = d_hidden_one * mixer_gain
    inner_one = width_total(jnp.sum(scaled_one * normed_one, axis=1, keepdims=True)) / D
    d_tokens = d_residual + scale_one * (scaled_one - normed_one * inner_one)
    gain_one_part = jnp.sum(d_hidden_one * normed_one, axis=0)
    grad_in, grad_out, grad_ffn, grad_down = (
        lax.psum(grad_in.astype(jnp.bfloat16), "dp").astype(jnp.float32),
        lax.psum(grad_out.astype(jnp.bfloat16), "dp").astype(jnp.float32),
        lax.psum(grad_ffn.astype(jnp.bfloat16), "dp").astype(jnp.float32),
        lax.psum(grad_down.astype(jnp.bfloat16), "dp").astype(jnp.float32),
    )
    gain_width = mixer_gain.shape[0]
    col_offset = lax.axis_index("col") * gain_width
    row_offset = lax.axis_index("row") * block_width
    zero_index = jnp.zeros((), jnp.int32)
    full_one = lax.dynamic_update_slice(jnp.zeros((D,), jnp.float32), gain_one_part, (col_offset,))
    full_two = lax.dynamic_update_slice(jnp.zeros((D,), jnp.float32), gain_two_part, (col_offset,))
    full_kernel = lax.dynamic_update_slice(
        jnp.zeros((3, D), jnp.float32), kernel_part, (zero_index, row_offset)
    )
    total_one, total_two, total_kernel = lax.psum(
        (full_one, full_two, full_kernel), ("dp", "row", "col")
    )
    grad_gain_one = lax.dynamic_slice_in_dim(total_one, col_offset, gain_width, 0)
    grad_gain_two = lax.dynamic_slice_in_dim(total_two, col_offset, gain_width, 0)
    grad_kernel = lax.dynamic_slice_in_dim(total_kernel, row_offset, block_width, 1)
    return (
        output,
        d_tokens,
        grad_gain_one,
        grad_in,
        grad_kernel,
        grad_out,
        grad_gain_two,
        grad_ffn,
        grad_down,
    )


def solution(mesh):
    in_specs = (
        P(("dp", "row"), "col"),
        P("col"),
        P("col", None, "row"),
        P(None, "row"),
        P("row", "col"),
        P("col"),
        P("col", None, "row"),
        P("row", "col"),
        P(("dp", "row"), "col"),
    )
    out_specs = (
        P(("dp", "row"), "col"),
        P(("dp", "row"), "col"),
        P("col"),
        P("col", None, "row"),
        P(None, "row"),
        P("row", "col"),
        P("col"),
        P("col", None, "row"),
        P("row", "col"),
    )
    return jax.shard_map(local, mesh=mesh, in_specs=in_specs, out_specs=out_specs, check_vma=False)
```

profile of v0, /device:TPU:0, one launch (start us, length us, event | category | flops | bytes accessed | tf_op | source)
XLA Modules:
  0.0 1960.4 jit_solution(6422226700840039610)
XLA Ops:
  8.9 5.9 psum.77
  20.6 32.4 %all-gather.9.cloned.1.call-done = bf16[2048,512]{1,0:T(8,128)(2,1)} async-done(((bf16[1024,512]{1,0:T(8,128)(2,1)}), bf16[2048,512]{1,0:T(8,128)(2,1)}) %all-gather.9.cloned.1.call-update) | async-done | bytes 2097168 | tf_op jit(solution)/shard_map/all_gather | solution.py:31
  52.9 10.0 fusion.20
  63.1 144.6 %reduce-scatter.9.cloned.1.call-done = f32[1024,1536]{1,0:T(8,128)} async-done(((f32[2048,1536]{1,0:T(8,128)}), f32[1024,1536]{1,0:T(8,128)}) %reduce-scatter.9.cloned.1.call-update) | async-done | bytes 6291472 | tf_op jit(solution)/shard_map/reduce_scatter | solution.py:44
  214.0 4.1 multiply_convert_fusion.7
  218.1 35.1 %all-gather.11.cloned.1.call-done = bf16[2048,512]{1,0:T(8,128)(2,1)} async-done(((bf16[1024,512]{1,0:T(8,128)(2,1)}), bf16[2048,512]{1,0:T(8,128)(2,1)}) %all-gather.11.cloned.1.call-update) | async-done | bytes 2097168 | tf_op jit(solution)/shard_map/all_gather | solution.py:35
  253.3 4.9 fusion.21
  258.8 53.9 %reduce-scatter.11.cloned.1.call-done = f32[1024,512]{1,0:T(8,128)} async-done(((f32[2048,512]{1,0:T(8,128)}), f32[1024,512]{1,0:T(8,128)}) %reduce-scatter.11.cloned.1.call-update) | async-done | bytes 2097168 | tf_op jit(solution)/shard_map/reduce_scatter | solution.py:58
  312.7 3.2 multiply_reduce_fusion.5
  315.9 4.9 psum.78
  320.9 3.0 multiply_convert_fusion.6
  324.0 23.2 %all-gather.17.cloned.1.call-done = bf16[2048,512]{1,0:T(8,128)(2,1)} async-done(((bf16[1024,512]{1,0:T(8,128)(2,1)}), bf16[2048,512]{1,0:T(8,128)(2,1)}) %all-gather.17.cloned.1.call-update) | async-done | bytes 2097168 | tf_op jit(solution)/shard_map/all_gather | solution.py:31
  347.2 11.5 fusion.24
  359.3 5.3 copy.22
  364.6 17.7 all-gather.13.cloned.1.call-done
  382.3 20.5 %fusion.22 = f32[2048,4608]{1,0:T(8,128)} fusion(bf16[2048,512]{1,0:T(8,128)(2,1)} %all-gather.13.cloned.1.call-done, bf16[512,4608]{1,0:T(8,128)(2,1)} %bitcast.44), kind=kOutput, calls=%fused_computation.62 | convolution fusion | flops 9663676416 | bytes 44564480 | tf_op jit(solution)/shard_map/dot_general | solution.py:21
  402.9 193.5 %reduce-scatter.17.cloned.1.call-done = f32[1024,2304]{1,0:T(8,128)} async-done(((f32[2048,2304]{1,0:T(8,128)}), f32[1024,2304]{1,0:T(8,128)}) %reduce-scatter.17.cloned.1.call-update) | async-done | bytes 9437200 | tf_op jit(solution)/shard_map/reduce_scatter | solution.py:44
  596.4 416.3 %reduce-scatter.13.cloned.1.call-done = f32[1024,4608]{1,0:T(8,128)} async-done(((f32[2048,4608]{1,0:T(8,128)}), f32[1024,4608]{1,0:T(8,128)}) %reduce-scatter.13.cloned.1.call-update) | async-done | bytes 18874384 | tf_op jit(solution)/shard_map/reduce_scatter | solution.py:44
  1012.7 13.4 multiply_convert_fusion.1
  1026.2 4.6 pad_maximum_fusion
  1030.8 224.4 %all-gather.19.cloned.1.call-done = bf16[2048,4608]{1,0:T(8,128)(2,1)} async-done(((bf16[1024,4608]{1,0:T(8,128)(2,1)}), bf16[2048,4608]{1,0:T(8,128)(2,1)}) %all-gather.19.cloned.1.call-update) | async-done | bytes 18874384 | tf_op jit(solution)/shard_map/all_gather | solution.py:35
  1255.2 16.5 fusion.25
  1271.8 54.5 %reduce-scatter.19.cloned.1.call-done = f32[1024,512]{1,0:T(8,128)} async-done(((f32[2048,512]{1,0:T(8,128)}), f32[1024,512]{1,0:T(8,128)}) %reduce-scatter.19.cloned.1.call-update) | async-done | bytes 2097168 | tf_op jit(solution)/shard_map/reduce_scatter | solution.py:58
  1329.1 4.9 psum.79
  1334.0 3.8 fusion.17
  1337.9 33.2 %all-gather.21.cloned.1.call-done = bf16[2048,512]{1,0:T(8,128)(2,1)} async-done(((bf16[1024,512]{1,0:T(8,128)(2,1)}), bf16[2048,512]{1,0:T(8,128)(2,1)}) %all-gather.21.cloned.1.call-update) | async-done | bytes 2097168 | tf_op jit(solution)/shard_map/all_gather | solution.py:31
  1371.1 5.0 fusion.26
  1376.9 53.7 %reduce-scatter.21.cloned.1.call-done = f32[1024,512]{1,0:T(8,128)} async-done(((f32[2048,512]{1,0:T(8,128)}), f32[1024,512]{1,0:T(8,128)}) %reduce-scatter.21.cloned.1.call-update) | async-done | bytes 2097168 | tf_op jit(solution)/shard_map/reduce_scatter | solution.py:44
  1430.6 5.3 multiply_reduce_fusion.3
  1437.4 4.0 collective-permute-done.1
  1448.3 101.9 %all-gather.15.cloned.1.call-done = bf16[2048,2304]{1,0:T(8,128)(2,1)} async-done(((bf16[1024,2304]{1,0:T(8,128)(2,1)}), bf16[2048,2304]{1,0:T(8,128)(2,1)}) %all-gather.15.cloned.1.call-update) | async-done | bytes 9437200 | tf_op jit(solution)/shard_map/all_gather | solution.py:35
  1550.2 10.5 convolution_convert_fusion.1
  1560.7 16.5 convolution_convert_fusion
  1577.2 7.2 convert_element_type.70
  1584.4 4.3 convolution_convert_fusion.3
  1588.7 43.9 %all-gather.23.cloned.1.call-done = bf16[2048,1536]{1,0:T(8,128)(2,1)} async-done(((bf16[1024,1536]{1,0:T(8,128)(2,1)}), bf16[2048,1536]{1,0:T(8,128)(2,1)}) %all-gather.23.cloned.1.call-update) | async-done | bytes 6291472 | tf_op jit(solution)/shard_map/all_gather | solution.py:35
  1632.5 8.0 convolution_convert_fusion.2
  1643.4 8.7 fusion.27
  1652.2 10.4 fusion.23
  1662.9 170.8 %all-reduce.4.cloned.1.call-done = (bf16[512,3,512]{0,2,1:T(8,128)(2,1)}, bf16[512,512]{1,0:T(8,128)(2,1)}, bf16[512,2,2304]{2,1,0:T(2,128)(2,1)}, bf16[2304,512]{1,0:T(8,128)(2,1)}) async-done(((bf16[512,3,512]{0,2,1:T(8,128)(2,1)}, bf16[512,512]{1,0:T(8,128)(2,1)}, bf16[512,2,2304]{2,1,0:T(2,128)(2,1)}, bf16[2304,512]{1,0:T(8,128)(2,1)}), (bf16[512,3,512]{0,2,1:T(8,128)(2,1)}, bf16[512,512]{1,0:T(8,128)(2,1)}, ...) | async-done | bytes 9175056 | tf_op jit(solution)/shard_map/psum | solution.py:160
  1833.7 7.4 convert_element_type.71
  1841.1 2.9 convert_element_type.73
  1844.0 3.2 copy.21
  1849.3 41.1 %reduce-scatter.23.cloned.1.call-done = f32[1024,512]{1,0:T(8,128)} async-done(((f32[2048,512]{1,0:T(8,128)}), f32[1024,512]{1,0:T(8,128)}) %reduce-scatter.23.cloned.1.call-update) | async-done | bytes 2097168 | tf_op jit(solution)/shard_map/reduce_scatter | solution.py:58
  1892.9 40.3 %all-reduce = (f32[1024]{0:T(1024)S(1)}, f32[3,1024]{1,0:T(4,128)S(1)}, f32[1024]{0:T(1024)S(1)}) all-reduce(f32[1024]{0:T(1024)S(1)} %dynamic_update_slice.9, f32[3,1024]{1,0:T(4,128)S(1)} %maximum_dynamic-update-slice_fusion, f32[1024]{0:T(1024)S(1)} %dynamic_update_slice.11), channel_id=1, replica_groups=mesh['dp'=8,'row'=2,'col'=2] {'dp','row','col'}, use_global_device_ids=true, to_apply=%region_17.0 | all-reduce | flops 5120 | bytes 40960 | tf_op jit(solution)/shard_map/psum | solution.py:174
  1934.6 5.1 psum.80
  1940.3 7.9 reduce-scatter.15.cloned.1.call-done
  1948.2 5.5 fusion.13
  (90 shorter events, 37.1 us)
Async XLA Ops:
  7.2 340.0 %copy-start = (bf16[2304,512]{1,0:T(8,128)(2,1)S(1)}, bf16[2304,512]{1,0:T(8,128)(2,1)}, u32[]{:S(2)}) copy-start(bf16[2304,512]{1,0:T(8,128)(2,1)} %param.16) | copy-start | bytes 7077892
  7.2 45.8 %all-gather.9.cloned.1.call-start = ((), (), s32[]{:S(2)}) async-start(), calls=%async_computation.8 | async-start | bytes 3145728 | tf_op jit(solution)/shard_map/all_gather | solution.py:31
  14.8 0.6 copy-start.7
  17.9 189.8 %reduce-scatter.9.cloned.1.call-start = ((), (), s32[]{:S(2)}) async-start(), calls=%async_computation.9 | async-start | bytes 18874368 | tf_op jit(solution)/shard_map/reduce_scatter | solution.py:44
  63.0 149.7 %copy-start.11 = (f32[3,512]{1,0:T(4,128)S(1)}, f32[3,512]{1,0:T(4,128)}, u32[]{:S(2)}) copy-start(f32[3,512]{1,0:T(4,128)} %param.12) | copy-start | bytes 18436
  63.0 190.3 %all-gather.11.cloned.1.call-start = ((), (), s32[]{:S(2)}) async-start(), calls=%async_computation.10 | async-start | bytes 3145728 | tf_op jit(solution)/shard_map/all_gather | solution.py:35
  210.4 7.7 copy-start.3
  210.4 3.6 collective-permute-start
  214.0 39.3 %copy-start.6 = (bf16[512,512]{1,0:T(8,128)(2,1)S(1)}, bf16[512,512]{1,0:T(8,128)(2,1)}, u32[]{:S(2)}) copy-start(bf16[512,512]{1,0:T(8,128)(2,1)} %param.13) | copy-start | bytes 1572868
  218.1 94.6 %reduce-scatter.11.cloned.1.call-start = ((), (), s32[]{:S(2)}) async-start(), calls=%async_computation.11 | async-start | bytes 6291456 | tf_op jit(solution)/shard_map/reduce_scatter | solution.py:58
  258.1 54.6 %copy-start.1 = (bf16[1024,512]{1,0:T(8,128)(2,1)S(1)}, bf16[1024,512]{1,0:T(8,128)(2,1)}, u32[]{:S(2)}) copy-start(bf16[1024,512]{1,0:T(8,128)(2,1)} %param.9) | copy-start | bytes 3145732
  258.2 89.0 %all-gather.17.cloned.1.call-start = ((), (), s32[]{:S(2)}) async-start(), calls=%async_computation.16 | async-start | bytes 3145728 | tf_op jit(solution)/shard_map/all_gather | solution.py:31
  258.7 62.1 %copy-start.9 = (f32[512]{0:T(512)S(1)}, f32[512]{0:T(512)}, u32[]{:S(2)}) copy-start(f32[512]{0:T(512)} %param.14) | copy-start | bytes 6148
  258.8 123.5 %all-gather.13.cloned.1.call-start = ((), (), s32[]{:S(2)}) async-start(), calls=%async_computation.12 | async-start | bytes 3145728 | tf_op jit(solution)/shard_map/all_gather | solution.py:31
  323.9 272.5 %reduce-scatter.17.cloned.1.call-start = ((), (), s32[]{:S(2)}) async-start(), calls=%async_computation.17 | async-start | bytes 28311552 | tf_op jit(solution)/shard_map/reduce_scatter | solution.py:44
  358.8 653.9 %reduce-scatter.13.cloned.1.call-start = ((), (), s32[]{:S(2)}) async-start(), calls=%async_computation.13 | async-start | bytes 56623104 | tf_op jit(solution)/shard_map/reduce_scatter | solution.py:44
  402.8 852.4 %all-gather.19.cloned.1.call-start = ((), (), s32[]{:S(2)}) async-start(), calls=%async_computation.18 | async-start | bytes 28311552 | tf_op jit(solution)/shard_map/all_gather | solution.py:35
  1030.7 295.5 %reduce-scatter.19.cloned.1.call-start = ((), (), s32[]{:S(2)}) async-start(), calls=%async_computation.19 | async-start | bytes 6291456 | tf_op jit(solution)/shard_map/reduce_scatter | solution.py:58
  1271.7 62.3 %copy-start.4 = (bf16[1024,512]{1,0:T(8,128)(2,1)S(1)}, bf16[1024,512]{1,0:T(8,128)(2,1)}, u32[]{:S(2)}) copy-start(bf16[1024,512]{1,0:T(8,128)(2,1)} %param.17) | copy-start | bytes 3145732
  1271.7 99.4 %all-gather.21.cloned.1.call-start = ((), (), s32[]{:S(2)}) async-start(), calls=%async_computation.20 | async-start | bytes 3145728 | tf_op jit(solution)/shard_map/all_gather | solution.py:31
  1337.8 92.8 %reduce-scatter.21.cloned.1.call-start = ((), (), s32[]{:S(2)}) async-start(), calls=%async_computation.21 | async-start | bytes 6291456 | tf_op jit(solution)/shard_map/reduce_scatter | solution.py:44
  1376.1 174.1 %all-gather.15.cloned.1.call-start = ((), (), s32[]{:S(2)}) async-start(), calls=%async_computation.14 | async-start | bytes 14155776 | tf_op jit(solution)/shard_map/all_gather | solution.py:35
  1376.8 255.7 %all-gather.23.cloned.1.call-start = ((), (), s32[]{:S(2)}) async-start(), calls=%async_computation.22 | async-start | bytes 9437184 | tf_op jit(solution)/shard_map/all_gather | solution.py:35
  1435.9 5.5 collective-permute-start.1
  1448.3 385.5 %all-reduce.4.cloned.1.call-start = ((), (), s32[]{:S(2)}) async-start(), calls=%async_computation.24 | async-start | bytes 18350080 | tf_op jit(solution)/shard_map/psum | solution.py:160
  1550.2 10.5 copy-start.12
  1643.2 247.2 %reduce-scatter.23.cloned.1.call-start = ((), (), s32[]{:S(2)}) async-start(), calls=%async_computation.23 | async-start | bytes 6291456 | tf_op jit(solution)/shard_map/reduce_scatter | solution.py:58
  1652.2 296.0 %reduce-scatter.15.cloned.1.call-start = ((), (), s32[]{:S(2)}) async-start(), calls=%async_computation.15 | async-start | bytes 6291456 | tf_op jit(solution)/shard_map/reduce_scatter | solution.py:58
  1833.7 7.4 copy-start.5
  1844.0 46.4 %copy-start.2 = (bf16[1024,512]{1,0:T(8,128)(2,1)S(1)}, bf16[1024,512]{1,0:T(8,128)(2,1)}, u32[]{:S(2)}) copy-start(bf16[1024,512]{1,0:T(8,128)(2,1)} %param.9) | copy-start | bytes 3145732
  1844.0 46.4 %copy-start.8 = (f32[1024,1]{0,1:T(1,128)S(1)}, f32[1024,1]{0,1:T(1,128)}, u32[]{:S(2)}) copy-start(f32[1024,1]{0,1:T(1,128)} %copy-done.7) | copy-start | bytes 12292
  1844.0 46.4 %copy-start.10 = (f32[512]{0:T(512)S(1)}, f32[512]{0:T(512)}, u32[]{:S(2)}) copy-start(f32[512]{0:T(512)} %param.10) | copy-start | bytes 6148
Sparse Core Ops, SparseCore 0:
  18.1 34.8 all-gather.8
  63.1 144.5 reduce-scatter.8
  218.2 35.0 all-gather.10
  258.3 54.3 reduce-scatter.10
  314.1 33.0 all-gather.16
  349.2 33.0 all-gather.12
  384.6 211.7 reduce-scatter.16
  598.7 413.9 reduce-scatter.12
  1030.9 224.3 all-gather.18
  1271.8 54.3 reduce-scatter.18
  1337.9 33.0 all-gather.20
  1376.2 54.3 reduce-scatter.20
  1432.2 117.9 all-gather.14
  1552.2 80.3 all-gather.22
  1643.3 190.3 all-reduce.3
  1835.9 54.4 reduce-scatter.22
  1892.6 55.5 reduce-scatter.14
where the time goes:
time: 1970 us; the launch traced here: 1960 us
  waiting for transfers between devices  1660 us (84%)
  matrix products  127 us (6%)
  other arithmetic  74.1 us (4%)
  blocking collectives  61.2 us (3%)
  local copies, waits for them, and re-layouts  23.9 us (1%)
    reduce_scatter x4, waiting for transfers between devices, spread_wide(): lax.psum_scatter(partial_rows(jnp.int32(0), height * lax.axis_size('col')...  808 us
    all_gather x4, waiting for transfers between devices, tokens_by_col(): return lax.all_gather(value, 'col', axis=0, tiled=True)  405 us
    psum x1, waiting for transfers between devices, local(): lax.psum(grad_in.astype(jnp.bfloat16), 'dp').astype(jnp.float32)  171 us
    reduce_scatter x4, waiting for transfers between devices, spread_narrow(): lax.psum_scatter(partial_rows(jnp.int32(0), height * lax.axis_size('row')...  157 us
    all_gather x4, waiting for transfers between devices, tokens_by_row(): return lax.all_gather(value, 'row', axis=0, tiled=True)  107 us
    dot_general x4, matrix products, dense(): return jnp.dot(left, matrix, preferred_element_type=jnp.float32)  45.8 us
    dot_general x4, matrix products, dense(): lax.dot_general(left, matrix, (((1,), (1,)), ((), ())), preferred_element...  41.7 us
    psum x1, blocking collectives, local(): lax.psum((full_one, full_two, full_kernel), ('dp', 'row', 'col'))  40.3 us
  transfers between devices with their start and end apart: 19, of which 19 were waited for; matrix products, arithmetic and copies ran while one was open for 7% of the time, Pallas kernels for 0%

commit v1 on v0

--- a/solution.py
+++ b/solution.py
@@ -5,6 +5,18 @@
 
 D = 1024
 EPS = 1e-05
+
+
+def unite_task(xin, axis_tag):
+    return jnp.concatenate(
+        lax.all_to_all(
+            jnp.stack([xin for _ in range(lax.psum(1, axis_tag))]),
+            axis_name=axis_tag,
+            split_axis=0,
+            concat_axis=0,
+        ),
+        axis=0,
+    )
 
 
 def shifted(block, axis, distance):
@@ -32,7 +44,7 @@
 
 
 def tokens_by_col(value):
-    return lax.all_gather(value, "col", axis=0, tiled=True)
+    return unite_task(value, "col")
 
 
 def spread_wide(gathered, matrix, transposed):

time: 1970 us -> 1930 us (0.980)
  waiting for transfers between devices: 1660 us -> 1340 us
  blocking collectives: 61.2 us -> 300 us
  local copies, waits for them, and re-layouts: 23.9 us -> 56.9 us
    all_gather x4 -> x0, waiting for transfers between devices: 405 us -> none  [tokens_by_col(): return lax.all_gather(value, 'col', axis=0, tiled=True)]
    all_to_all x0 -> x2, blocking collectives: none -> 238 us  [unite_task(): lax.all_to_all(jnp.stack([xin for _ in range(lax.psum(1, axis_tag))]), ax...]
    ppermute x2, waiting for transfers between devices: 5.31 us -> 59.9 us  [shifted(): return lax.ppermute(block, axis, route)]
    dot_general x0 -> x2, local copies, waits for them, and re-layouts: none -> 33.5 us  [grads_of(): lax.dot_general(left, right, (((0,), (0,)), ((), ())), preferred_element_...]
  transfers between devices with their start and end apart: 19 -> 17, of which waited for: 19 -> 16; matrix products, arithmetic and copies ran while one was open for 7% -> 8% of each run, Pallas kernels for 0% -> 0%
where the time goes in v1:
time: 1930 us; the launch traced here: 1920 us
  waiting for transfers between devices  1340 us (69%)
  blocking collectives  300 us (16%)
  matrix products  121 us (6%)
  other arithmetic  75.4 us (4%)
  local copies, waits for them, and re-layouts  56.9 us (3%)
    reduce_scatter x4, waiting for transfers between devices, spread_wide(): lax.psum_scatter(partial_rows(jnp.int32(0), height * lax.axis_size('col')...  828 us
    all_to_all x2, blocking collectives, unite_task(): lax.all_to_all(jnp.stack([xin for _ in range(lax.psum(1, axis_tag))]), ax...  238 us
    psum x1, waiting for transfers between devices, local(): lax.psum(grad_ffn.astype(jnp.bfloat16), 'dp').astype(jnp.float32)  171 us
    reduce_scatter x4, waiting for transfers between devices, spread_narrow(): lax.psum_scatter(partial_rows(jnp.int32(0), height * lax.axis_size('row')...  156 us
    all_gather x4, waiting for transfers between devices, tokens_by_row(): return lax.all_gather(value, 'row', axis=0, tiled=True)  106 us
    ppermute x2, waiting for transfers between devices, shifted(): return lax.ppermute(block, axis, route)  59.9 us
    dot_general x4, matrix products, dense(): return jnp.dot(left, matrix, preferred_element_type=jnp.float32)  44.1 us
    psum x1, blocking collectives, local(): lax.psum((full_one, full_two, full_kernel), ('dp', 'row', 'col'))  40.5 us
  transfers between devices with their start and end apart: 17, of which 16 were waited for; matrix products, arithmetic and copies ran while one was open for 8% of the time, Pallas kernels for 0%

profile of v1, /device:TPU:0, one launch (start us, length us, event | category | flops | bytes accessed | tf_op | source)
XLA Modules:
  0.0 1924.2 jit_solution(8212097030614542255)
XLA Ops:
  8.9 5.9 psum.77
  20.6 32.4 %all-gather.5.cloned.1.call-done = bf16[2048,512]{1,0:T(8,128)(2,1)} async-done(((bf16[1024,512]{1,0:T(8,128)(2,1)}), bf16[2048,512]{1,0:T(8,128)(2,1)}) %all-gather.5.cloned.1.call-update) | async-done | bytes 2097168 | tf_op jit(solution)/shard_map/all_gather | solution.py:43
  52.9 10.0 fusion.33
  63.1 144.6 %reduce-scatter.9.cloned.1.call-done = f32[1024,1536]{1,0:T(8,128)} async-done(((f32[2048,1536]{1,0:T(8,128)}), f32[1024,1536]{1,0:T(8,128)}) %reduce-scatter.9.cloned.1.call-update) | async-done | bytes 6291472 | tf_op jit(solution)/shard_map/reduce_scatter | solution.py:56
  214.0 3.7 fusion.26
  217.9 27.2 %all_to_all.20 = bf16[2,1024,512]{2,1,0:T(8,128)(2,1)S(1)} all-to-all(bf16[2,1024,512]{2,1,0:T(8,128)(2,1)S(1)} %pad_maximum_fusion.3), channel_id=1, replica_groups=mesh['dp'=8,'row'=2,'col'=2] {'col'}, dimensions={0} | all-to-all | bytes 4194304 | tf_op jit(solution)/shard_map/all_to_all | solution.py:12
  246.6 3.3 fusion.34
  250.5 53.9 %reduce-scatter.11.cloned.1.call-done = f32[1024,512]{1,0:T(8,128)} async-done(((f32[2048,512]{1,0:T(8,128)}), f32[1024,512]{1,0:T(8,128)}) %reduce-scatter.11.cloned.1.call-update) | async-done | bytes 2097168 | tf_op jit(solution)/shard_map/reduce_scatter | solution.py:70
  304.4 3.2 multiply_reduce_fusion.5
  307.7 4.9 psum.78
  312.6 3.0 multiply_convert_fusion.6
  315.7 23.3 %all-gather.9.cloned.1.call-done = bf16[2048,512]{1,0:T(8,128)(2,1)} async-done(((bf16[1024,512]{1,0:T(8,128)(2,1)}), bf16[2048,512]{1,0:T(8,128)(2,1)}) %all-gather.9.cloned.1.call-update) | async-done | bytes 2097168 | tf_op jit(solution)/shard_map/all_gather | solution.py:43
  339.0 11.5 fusion.37
  351.1 5.3 copy.33
  356.4 17.7 all-gather.7.cloned.1.call-done
  374.1 20.4 %fusion.35 = f32[2048,4608]{1,0:T(8,128)} fusion(bf16[2048,512]{1,0:T(8,128)(2,1)} %all-gather.7.cloned.1.call-done, bf16[512,4608]{1,0:T(8,128)(2,1)} %bitcast.78), kind=kOutput, calls=%fused_computation.74 | convolution fusion | flops 9663676416 | bytes 44564480 | tf_op jit(solution)/shard_map/dot_general | solution.py:33
  394.6 193.5 %reduce-scatter.17.cloned.1.call-done = f32[1024,2304]{1,0:T(8,128)} async-done(((f32[2048,2304]{1,0:T(8,128)}), f32[1024,2304]{1,0:T(8,128)}) %reduce-scatter.17.cloned.1.call-update) | async-done | bytes 9437200 | tf_op jit(solution)/shard_map/reduce_scatter | solution.py:56
  588.0 416.3 %reduce-scatter.13.cloned.1.call-done = f32[1024,4608]{1,0:T(8,128)} async-done(((f32[2048,4608]{1,0:T(8,128)}), f32[1024,4608]{1,0:T(8,128)}) %reduce-scatter.13.cloned.1.call-update) | async-done | bytes 18874384 | tf_op jit(solution)/shard_map/reduce_scatter | solution.py:56
  1004.3 13.5 fusion.2
  1017.8 3.6 maximum_maximum_fusion
  1021.4 211.1 %all_to_all.21 = bf16[2,1024,4608]{2,1,0:T(8,128)(2,1)} all-to-all(bf16[2,1024,4608]{2,1,0:T(8,128)(2,1)S(1)} %maximum_maximum_fusion), channel_id=1, replica_groups=mesh['dp'=8,'row'=2,'col'=2] {'col'}, dimensions={0} | all-to-all | bytes 37748736 | tf_op jit(solution)/shard_map/all_to_all | solution.py:12
  1232.5 15.1 fusion.38
  1247.7 54.4 %reduce-scatter.19.cloned.1.call-done = f32[1024,512]{1,0:T(8,128)} async-done(((f32[2048,512]{1,0:T(8,128)}), f32[1024,512]{1,0:T(8,128)}) %reduce-scatter.19.cloned.1.call-update) | async-done | bytes 2097168 | tf_op jit(solution)/shard_map/reduce_scatter | solution.py:70
  1305.0 4.9 psum.79
  1309.9 3.8 fusion.30
  1313.9 33.0 %all-gather.11.cloned.1.call-done = bf16[2048,512]{1,0:T(8,128)(2,1)} async-done(((bf16[1024,512]{1,0:T(8,128)(2,1)}), bf16[2048,512]{1,0:T(8,128)(2,1)}) %all-gather.11.cloned.1.call-update) | async-done | bytes 2097168 | tf_op jit(solution)/shard_map/all_gather | solution.py:43
  1347.0 5.0 fusion.39
  1352.0 8.5 pad_maximum_fusion
  1360.4 7.4 all-to-all-start.1
  1367.8 73.2 %reduce-scatter.21.cloned.1.call-done = f32[1024,512]{1,0:T(8,128)} async-done(((f32[2048,512]{1,0:T(8,128)}), f32[1024,512]{1,0:T(8,128)}) %reduce-scatter.21.cloned.1.call-update) | async-done | bytes 2097168 | tf_op jit(solution)/shard_map/reduce_scatter | solution.py:56
  1441.0 5.3 multiply_reduce_fusion.3
  1447.7 58.6 %collective-permute-done.1 = f32[2,512]{1,0:T(2,128)S(1)} collective-permute-done((f32[2,512]{1,0:T(2,128)S(1)}, f32[2,512]{1,0:T(2,128)S(1)}, u32[]{:S(2)}, u32[]{:S(2)}) %collective-permute-start.1) | collective-permute-done | bytes 4128 | tf_op jit(solution)/shard_map/ppermute | solution.py:25
  1513.5 6.2 all-to-all-start.3
  1519.8 10.4 convolution_convert_fusion.1
  1530.2 24.7 %copy.26 = bf16[4608,2048]{1,0:T(8,128)(2,1)} copy(bf16[4608,2048]{0,1:T(8,128)(2,1)} %bitcast.72) | data formatting | bytes 37748736 | tf_op jit(solution)/shard_map/dot_general | solution.py:37
  1554.9 16.1 convolution_convert_fusion
  1573.1 16.8 all-to-all-done.3
  1589.8 8.8 copy.24
  1598.6 8.0 fusion.23
  1606.7 8.7 fusion.40
  1615.5 10.4 fusion.36
  1626.2 171.1 %all-reduce.4.cloned.1.call-done = (bf16[512,2,2304]{2,0,1:T(8,128)(2,1)}, bf16[512,3,512]{2,0,1:T(8,128)(2,1)}, bf16[512,512]{1,0:T(8,128)(2,1)}, bf16[2304,512]{1,0:T(8,128)(2,1)}) async-done(((bf16[512,2,2304]{2,0,1:T(8,128)(2,1)}, bf16[512,3,512]{2,0,1:T(8,128)(2,1)}, bf16[512,512]{1,0:T(8,128)(2,1)}, bf16[2304,512]{1,0:T(8,128)(2,1)}), (bf16[512,2,2304]{2,0,1:T(8,128)(2,1)}, ...) | async-done | bytes 9175056 | tf_op jit(solution)/shard_map/psum | solution.py:174
  1797.2 10.8 copy.28
  1814.2 39.7 %reduce-scatter.23.cloned.1.call-done = f32[1024,512]{1,0:T(8,128)} async-done(((f32[2048,512]{1,0:T(8,128)}), f32[1024,512]{1,0:T(8,128)}) %reduce-scatter.23.cloned.1.call-update) | async-done | bytes 2097168 | tf_op jit(solution)/shard_map/reduce_scatter | solution.py:70
  1856.4 40.5 %all-reduce = (f32[1024]{0:T(1024)S(1)}, f32[3,1024]{1,0:T(4,128)S(1)}, f32[1024]{0:T(1024)S(1)}) all-reduce(f32[1024]{0:T(1024)S(1)} %dynamic_update_slice.9, f32[3,1024]{1,0:T(4,128)S(1)} %maximum_dynamic-update-slice_fusion, f32[1024]{0:T(1024)S(1)} %dynamic_update_slice.11), channel_id=1, replica_groups=mesh['dp'=8,'row'=2,'col'=2] {'dp','row','col'}, use_global_device_ids=true, to_apply=%region_17.0 | all-reduce | flops 5120 | bytes 40960 | tf_op jit(solution)/shard_map/psum | solution.py:186
  1898.3 5.1 psum.80
  1904.0 7.8 reduce-scatter.15.cloned.1.call-done
  1911.8 5.5 fusion.16
  (99 shorter events, 41.4 us)
Async XLA Ops:
  7.2 331.8 %copy-start = (bf16[2304,512]{1,0:T(8,128)(2,1)S(1)}, bf16[2304,512]{1,0:T(8,128)(2,1)}, u32[]{:S(2)}) copy-start(bf16[2304,512]{1,0:T(8,128)(2,1)} %param.16) | copy-start | bytes 7077892
  7.2 45.8 %all-gather.5.cloned.1.call-start = ((), (), s32[]{:S(2)}) async-start(), calls=%async_computation.12 | async-start | bytes 3145728 | tf_op jit(solution)/shard_map/all_gather | solution.py:43
  14.8 0.6 copy-start.12
  17.9 189.8 %reduce-scatter.9.cloned.1.call-start = ((), (), s32[]{:S(2)}) async-start(), calls=%async_computation.13 | async-start | bytes 18874368 | tf_op jit(solution)/shard_map/reduce_scatter | solution.py:56
  63.0 149.7 %copy-start.16 = (f32[3,512]{1,0:T(4,128)S(1)}, f32[3,512]{1,0:T(4,128)}, u32[]{:S(2)}) copy-start(f32[3,512]{1,0:T(4,128)} %param.12) | copy-start | bytes 18436
  63.0 241.4 %reduce-scatter.11.cloned.1.call-start = ((), (), s32[]{:S(2)}) async-start(), calls=%async_computation.14 | async-start | bytes 6291456 | tf_op jit(solution)/shard_map/reduce_scatter | solution.py:70
  210.4 7.3 copy-start.5
  210.4 3.6 collective-permute-start
  217.9 28.7 %copy-start.9 = (bf16[512,512]{1,0:T(8,128)(2,1)S(1)}, bf16[512,512]{1,0:T(8,128)(2,1)}, u32[]{:S(2)}) copy-start(bf16[512,512]{1,0:T(8,128)(2,1)} %param.13) | copy-start | bytes 1572868
  245.1 1.5 copy-start.3
  249.9 54.6 %copy-start.1 = (bf16[1024,512]{1,0:T(8,128)(2,1)S(1)}, bf16[1024,512]{1,0:T(8,128)(2,1)}, u32[]{:S(2)}) copy-start(bf16[1024,512]{1,0:T(8,128)(2,1)} %param.9) | copy-start | bytes 3145732
  249.9 89.1 %all-gather.9.cloned.1.call-start = ((), (), s32[]{:S(2)}) async-start(), calls=%async_computation.18 | async-start | bytes 3145728 | tf_op jit(solution)/shard_map/all_gather | solution.py:43
  250.5 62.1 %copy-start.14 = (f32[512]{0:T(512)S(1)}, f32[512]{0:T(512)}, u32[]{:S(2)}) copy-start(f32[512]{0:T(512)} %param.14) | copy-start | bytes 6148
  250.5 123.6 %all-gather.7.cloned.1.call-start = ((), (), s32[]{:S(2)}) async-start(), calls=%async_computation.15 | async-start | bytes 3145728 | tf_op jit(solution)/shard_map/all_gather | solution.py:43
  315.7 272.3 %reduce-scatter.17.cloned.1.call-start = ((), (), s32[]{:S(2)}) async-start(), calls=%async_computation.19 | async-start | bytes 28311552 | tf_op jit(solution)/shard_map/reduce_scatter | solution.py:56
  350.5 653.8 %reduce-scatter.13.cloned.1.call-start = ((), (), s32[]{:S(2)}) async-start(), calls=%async_computation.16 | async-start | bytes 56623104 | tf_op jit(solution)/shard_map/reduce_scatter | solution.py:56
  394.5 907.6 %reduce-scatter.19.cloned.1.call-start = ((), (), s32[]{:S(2)}) async-start(), calls=%async_computation.20 | async-start | bytes 6291456 | tf_op jit(solution)/shard_map/reduce_scatter | solution.py:70
  1017.8 214.7 %slice-start = ((s8[4718592]{0:T(1024)(128)(4,1)}), s8[524288]{0:T(1024)(128)(4,1)S(1)}, s32[]{:S(2)}) async-start(s8[4718592]{0:T(1024)(128)(4,1)} %bitcast.79), calls=%async_computation.25 | async-start | bytes 1048576
  1021.4 211.1 %slice-start.1 = ((s8[4718592]{0:T(1024)(128)(4,1)}), s8[4194304]{0:T(1024)(128)(4,1)S(1)}, s32[]{:S(2)}) async-start(s8[4718592]{0:T(1024)(128)(4,1)} %bitcast.79), calls=%async_computation.26 | async-start | bytes 8388608
  1247.6 62.3 %copy-start.7 = (bf16[1024,512]{1,0:T(8,128)(2,1)S(1)}, bf16[1024,512]{1,0:T(8,128)(2,1)}, u32[]{:S(2)}) copy-start(bf16[1024,512]{1,0:T(8,128)(2,1)} %param.17) | copy-start | bytes 3145732
  1247.6 99.3 %all-gather.11.cloned.1.call-start = ((), (), s32[]{:S(2)}) async-start(), calls=%async_computation.21 | async-start | bytes 3145728 | tf_op jit(solution)/shard_map/all_gather | solution.py:43
  1313.7 127.3 %reduce-scatter.21.cloned.1.call-start = ((), (), s32[]{:S(2)}) async-start(), calls=%async_computation.22 | async-start | bytes 6291456 | tf_op jit(solution)/shard_map/reduce_scatter | solution.py:56
  1360.4 153.1 %all-to-all-start.1 = ((bf16[2,1024,2304]{2,1,0:T(8,128)(2,1)}), bf16[2,1024,2304]{2,1,0:T(8,128)(2,1)}, u32[]{:S(2)}, u32[]{:S(2)}) async-start(bf16[2,1024,2304]{2,1,0:T(8,128)(2,1)} %pad_maximum_fusion), calls=%async_computation.4 | async-start | bytes 18874368 | tf_op jit(solution)/shard_map/all_to_all | solution.py:12
  1446.4 59.9 %collective-permute-start.1 = (f32[2,512]{1,0:T(2,128)S(1)}, f32[2,512]{1,0:T(2,128)S(1)}, u32[]{:S(2)}, u32[]{:S(2)}) collective-permute-start(f32[2,512]{1,0:T(2,128)S(1)} %slice.67), channel_id=1, source_target_pairs={{1,0},{3,2},{5,4},{7,6},{9,8},{11,10},{13,12},{15,14},{17,16},{19,... | collective-permute-start | bytes 12296 | tf_op jit(solution)/shard_map/ppermute | solution.py:25
  1513.5 76.3 %all-to-all-start.3 = ((bf16[2,1024,1536]{2,1,0:T(8,128)(2,1)}), bf16[2,1024,1536]{2,1,0:T(8,128)(2,1)}, u32[]{:S(2)}, u32[]{:S(2)}) async-start(bf16[2,1024,1536]{2,1,0:T(8,128)(2,1)} %maximum_maximum_fusion.1), calls=%async_computation.10 | async-start | bytes 12582912 | tf_op jit(solution)/shard_map/all_to_all | solution.py:12
  1519.7 277.5 %all-reduce.4.cloned.1.call-start = ((), (), s32[]{:S(2)}) async-start(), calls=%async_computation.24 | async-start | bytes 18350080 | tf_op jit(solution)/shard_map/psum | solution.py:174
  1554.9 16.1 copy-start.4
  1554.9 16.1 copy-start.6
  1606.7 247.2 %reduce-scatter.23.cloned.1.call-start = ((), (), s32[]{:S(2)}) async-start(), calls=%async_computation.23 | async-start | bytes 6291456 | tf_op jit(solution)/shard_map/reduce_scatter | solution.py:70
  1615.4 296.4 %reduce-scatter.15.cloned.1.call-start = ((), (), s32[]{:S(2)}) async-start(), calls=%async_computation.17 | async-start | bytes 6291456 | tf_op jit(solution)/shard_map/reduce_scatter | solution.py:70
  1797.2 10.9 copy-start.8
  1808.1 2.9 copy-start.10
  1810.9 2.1 copy-start.11
  1810.9 43.0 %copy-start.2 = (bf16[1024,512]{1,0:T(8,128)(2,1)S(1)}, bf16[1024,512]{1,0:T(8,128)(2,1)}, u32[]{:S(2)}) copy-start(bf16[1024,512]{1,0:T(8,128)(2,1)} %param.9) | copy-start | bytes 3145732
  1810.9 43.0 %copy-start.13 = (f32[1024,1]{0,1:T(1,128)S(1)}, f32[1024,1]{0,1:T(1,128)}, u32[]{:S(2)}) copy-start(f32[1024,1]{0,1:T(1,128)} %copy-done.12) | copy-start | bytes 12292
  1811.0 43.0 %copy-start.15 = (f32[512]{0:T(512)S(1)}, f32[512]{0:T(512)}, u32[]{:S(2)}) copy-start(f32[512]{0:T(512)} %param.10) | copy-start | bytes 6148
Sparse Core Ops, SparseCore 0:
  18.1 34.8 all-gather.4
  63.1 144.5 reduce-scatter.8
  250.0 54.3 reduce-scatter.10
  305.8 33.0 all-gather.8
  340.9 33.0 all-gather.6
  376.2 211.7 reduce-scatter.16
  590.3 413.9 reduce-scatter.12
  1247.7 54.3 reduce-scatter.18
  1313.8 33.0 all-gather.10
  1352.1 88.9 reduce-scatter.20
  1606.8 190.3 all-reduce.3
  1799.4 54.4 reduce-scatter.22
  1856.2 55.6 reduce-scatter.14
